TPU v7x, 32 devices: a whole 2x2x4 slice. The times are simulated.
32 devices in a mesh: dp: 8 (over z, x), mp: 4 (over y, core).
Axes of the slice: x: 2, y: 2, z: 4, core: 2. Of those that a mesh axis runs over, the one named last changes fastest.
Arguments:
- tokens: bfloat16 [256, 48, 3584], P('dp', None, 'mp'), may hold values from -180 to 180
- norm_gain: float32 [3584], replicated, may hold values from 0.1 to 1.9
- w_query: bfloat16 [3584, 3584], P('dp', 'mp'), may hold values from -0.16 to 0.16
- w_keyval: bfloat16 [3584, 2, 512], P('dp', None, 'mp'), may hold values from -0.16 to 0.16
- w_out: bfloat16 [3584, 3584], P('mp', 'dp'), may hold values from -0.09375 to 0.09375
- residents: bfloat16 [8, 2048, 3584], P('dp', 'mp'), may hold values from -6 to 6
- lengths: int32 [256], P('dp'), may hold values from 6 to 48
- cluster: int32 [256, 1], P('dp'), may hold values from 0 to 7; in each aligned block of 32 rows (0 to 31, 32 to 63, ...) at most 4 rows name the same one
- owner: int32 [8], replicated, may hold values from 0 to 7, each once
- counts: int32 [8], replicated, may hold values from 256 to 2048
- flags: int32 [256], P('dp'), may hold values 0 or 1
Outputs:
- similarity: float32 [256, 2048], P('dp', 'mp')
Inputs may be any that keep to these rules, and one draw needn't show every extreme that they name: Each dialogue's cluster; among the 32 dialogues of one index of dp (aligned blocks of rows) no cluster is named more than 4 times. owner gives every cluster a distinct index of dp that holds its residents.
All inputs are finite; a program needn't handle non-finite values. No bound on the sum of `flags` on one device may be relied on, other than what follows from the above.
Results may differ from a plain program's by a relative error of at most 0.013.
Values may be sent and summed in bfloat16 or wider, within the bound.
A program may use at most 128 MiB of HBM per device.

v0:
```python
import math
import jax
import jax.numpy as jnp
from jax import lax
from jax.sharding import PartitionSpec as P

HEAD_DIM = 128
rope_base = 1000000.0
logit_scale = 100.0


def rotate(values, positions):
    half = values.shape[-1] // 2
    freqs = rope_base ** (-jnp.arange(half, dtype=jnp.float32) * 2.0 / values.shape[-1])
    angles = positions.astype(jnp.float32)[:, None] * freqs[None, :]
    cosine = jnp.cos(angles)[:, None, :]
    sine = jnp.sin(angles)[:, None, :]
    first = values[..., :half]
    second = values[..., half:]
    return jnp.concatenate(
        [first * cosine - second * sine, second * cosine + first * sine], axis=-1
    )


def attend(query, keys, values, length):
    seq_len = query.shape[0]
    kv_count = keys.shape[1]
    group = query.shape[1] // kv_count
    grouped = query.reshape(seq_len, kv_count, group, query.shape[-1])
    scores = jnp.einsum(
        "qkgd,pkd->kgqp", grouped, keys, preferred_element_type=jnp.float32
    ) / math.sqrt(query.shape[-1])
    row_pos = jnp.arange(seq_len)[:, None]
    col_pos = jnp.arange(seq_len)[None, :]
    allowed = (col_pos <= row_pos) & (col_pos < length)
    scores = jnp.where(allowed, scores, -1e30)
    highest = jnp.max(scores, axis=-1, keepdims=True)
    expanded = jnp.exp(scores - highest)
    weights = (expanded / jnp.sum(expanded, axis=-1, keepdims=True)).astype(jnp.bfloat16)
    context = jnp.einsum("kgqp,pkd->qkgd", weights, values, preferred_element_type=jnp.float32)
    valid = (jnp.arange(seq_len) < length).astype(jnp.float32)
    pooled = jnp.sum(context * valid[:, None, None, None], axis=0) / length.astype(jnp.float32)
    return pooled.reshape(-1)


def local(
    tokens, norm_gain, w_query, w_keyval, w_out, residents, lengths, cluster, owner, counts, flags
):
    gathered = lax.all_gather(tokens, "mp", axis=2, tiled=True)
    dialogs, seq_len, width = gathered.shape
    hidden = gathered.astype(jnp.float32)
    normed = (
        hidden * lax.rsqrt(jnp.mean(hidden * hidden, axis=-1, keepdims=True) + 1e-06) * norm_gain
    ).astype(jnp.bfloat16)
    normed_flat = normed.reshape(dialogs * seq_len, width)
    query_cols = w_query.shape[1]
    keyval_cols = w_keyval.shape[2]
    pieces = (
        lax.all_gather(w_query, "dp", axis=0, tiled=True),
        lax.all_gather(w_keyval, "dp", axis=0, tiled=True),
    )
    keyval_piece = pieces[1].reshape(pieces[1].shape[0], 2 * keyval_cols)
    query_sum = jnp.dot(normed_flat, pieces[0], preferred_element_type=jnp.float32)
    keyval_sum = jnp.dot(normed_flat, keyval_piece, preferred_element_type=jnp.float32)
    positions = jnp.arange(seq_len)
    local_heads = query_cols // HEAD_DIM
    local_kv = keyval_cols // HEAD_DIM
    query = jax.vmap(lambda block: rotate(block, positions))(
        query_sum.reshape(dialogs, seq_len, local_heads, HEAD_DIM)
    ).astype(jnp.bfloat16)
    keys = jax.vmap(lambda block: rotate(block, positions))(
        keyval_sum[:, :keyval_cols].reshape(dialogs, seq_len, local_kv, HEAD_DIM)
    ).astype(jnp.bfloat16)
    values = (
        keyval_sum[:, keyval_cols:]
        .reshape(dialogs, seq_len, local_kv, HEAD_DIM)
        .astype(jnp.bfloat16)
    )
    pooled_context = jax.vmap(attend)(query, keys, values, lengths).astype(jnp.bfloat16)
    valid = (positions[None, :] < lengths[:, None]).astype(jnp.float32)
    pooled_input = (
        jnp.sum(hidden * valid[:, :, None], axis=1) / lengths.astype(jnp.float32)[:, None]
    )
    partial_out = jnp.dot(
        pooled_context,
        lax.all_gather(w_out, "dp", axis=1, tiled=True),
        preferred_element_type=jnp.float32,
    )
    projected = lax.psum(partial_out.astype(jnp.bfloat16), "mp").astype(jnp.float32)
    embedding = pooled_input + projected
    unit = embedding * lax.rsqrt(jnp.sum(embedding * embedding, axis=-1, keepdims=True) + 1e-06)
    unit = (unit * flags.astype(jnp.float32)[:, None]).astype(jnp.bfloat16)
    my_index = lax.axis_index("dp")
    owner_count = lax.axis_size("dp")
    my_count = jnp.sum(jnp.where(owner == my_index, counts, 0))
    members = residents[0]
    member_count = members.shape[0]
    inverse_norm = lax.rsqrt(
        jnp.einsum("md,md->m", members, members, preferred_element_type=jnp.float32) + 1e-06
    )
    member_start = lax.axis_index("mp") * member_count
    live = member_start + jnp.arange(member_count) < my_count
    table_size = owner.shape[0]
    cluster_ids = cluster[:, 0]
    destination = jnp.sum(
        jnp.where(jnp.arange(table_size)[None, :] == cluster_ids[:, None], owner[None, :], 0),
        axis=1,
    )
    capacity = max(1, -(-dialogs // owner_count))
    order = jnp.arange(dialogs)
    earlier = (destination[None, :] == destination[:, None]) & (order[None, :] < order[:, None])
    rank = jnp.sum(earlier.astype(jnp.int32), axis=1)
    onehot = (jnp.arange(owner_count)[:, None, None] == destination[None, None, :]) & (
        jnp.arange(capacity)[None, :, None] == rank[None, None, :]
    )
    outgoing = jnp.einsum(
        "ocn,nd->ocd", onehot.astype(jnp.bfloat16), unit, preferred_element_type=jnp.float32
    ).astype(jnp.bfloat16)
    query_rows = lax.all_to_all(outgoing, "dp", split_axis=0, concat_axis=0, tiled=True)
    dots = lax.dot_general(
        query_rows,
        members,
        (((query_rows.ndim - 1,), (1,)), ((), ())),
        preferred_element_type=jnp.float32,
    )
    returned = lax.all_to_all(
        jnp.where(live, logit_scale * dots * inverse_norm, 0.0).astype(jnp.bfloat16),
        "dp",
        split_axis=0,
        concat_axis=0,
        tiled=True,
    ).astype(jnp.float32)
    similarity = jnp.einsum(
        "ocn,ocm->nm", onehot.astype(jnp.float32), returned, precision=lax.Precision.HIGHEST
    )
    return similarity


def solution(mesh):
    in_specs = (
        P("dp", None, "mp"),
        P(),
        P("dp", "mp"),
        P("dp", None, "mp"),
        P("mp", "dp"),
        P("dp", "mp", None),
        P("dp"),
        P("dp", None),
        P(),
        P(),
        P("dp"),
    )
    out_specs = P("dp", "mp")
    return jax.shard_map(local, mesh=mesh, in_specs=in_specs, out_specs=out_specs, check_vma=False)
```

profile of v0, /device:TPU:0, one launch (start us, length us, event | category | flops | bytes accessed | tf_op | source)
XLA Modules:
  0.0 408.5 jit_solution(2310838354348667568)
XLA Ops:
  12.9 2.8 fusion.6
  15.7 97.3 %all-gather.9.cloned.1.call-done = bf16[3584,896]{1,0:T(8,128)(2,1)} async-done(((bf16[448,896]{1,0:T(8,128)(2,1)}), bf16[3584,896]{1,0:T(8,128)(2,1)}) %all-gather.9.cloned.1.call-update) | async-done | bytes 6422544 | tf_op jit(solution)/shard_map/all_gather | solution.py:59
  113.0 9.7 %copy.20 = bf16[896,3584]{1,0:T(8,128)(2,1)} copy(bf16[896,3584]{0,1:T(8,128)(2,1)} %bitcast.86) | data formatting | bytes 12845056 | tf_op jit(solution)/shard_map/dot_general | solution.py:63
  122.7 63.2 %all-gather.5.cloned.1.call-done = bf16[32,48,3584]{2,1,0:T(8,128)(2,1)} async-done(((bf16[32,48,896]{2,1,0:T(8,128)(2,1)}), bf16[32,48,3584]{2,1,0:T(8,128)(2,1)}) %all-gather.5.cloned.1.call-update) | async-done | bytes 11010064 | tf_op jit(solution)/shard_map/all_gather | solution.py:49
  185.8 8.9 %fusion = (f32[32,3584]{1,0:T(8,128)S(1)}, f32[32,48]{1,0:T(8,128)S(1)}) fusion(bf16[32,48,3584]{2,1,0:T(8,128)(2,1)} %all-gather.5.cloned.1.call-done, f32[32,48]{1,0:T(8,128)S(1)} %get-tuple-element.14), kind=kLoop, calls=%fused_computation.3 | loop fusion | flops 27408896 | bytes 11481088 | tf_op jit(solution)/shard_map/reduce_sum | solution.py:82
  194.8 11.0 %fusion.3 = bf16[32,48,3584]{2,1,0:T(8,128)(2,1)} fusion(bf16[32,48,3584]{2,1,0:T(8,128)(2,1)} %all-gather.5.cloned.1.call-done, f32[3584]{0:T(1024)S(1)} %copy-done.1, f32[32,48]{1,0:T(8,128)S(1)} %add_rsqrt_fusion), kind=kLoop, calls=%fused_computation.6 | loop fusion | flops 22020096 | bytes 22040576 | tf_op jit(solution)/shard_map/convert_element_type | solution.py:54
  205.7 28.8 %all-gather.7.cloned.1.call-done = bf16[3584,2,128]{2,1,0:T(2,128)(2,1)} async-done(((bf16[448,2,128]{2,1,0:T(2,128)(2,1)}), bf16[3584,2,128]{2,1,0:T(2,128)(2,1)}) %all-gather.7.cloned.1.call-update) | async-done | bytes 1835024 | tf_op jit(solution)/shard_map/all_gather | solution.py:60
  234.5 7.2 %fusion.22 = f32[1536,256]{1,0:T(8,128)S(1)} fusion(bf16[1536,3584]{1,0:T(8,128)(2,1)} %bitcast.84, bf16[448,8,2,128]{3,2,1,0:T(2,128)(2,1)} %bitcast.92), kind=kOutput, calls=%fused_computation.34 | convolution fusion | flops 2818572288 | bytes 14417920 | tf_op jit(solution)/shard_map/dot_general | solution.py:64
  242.4 1.5 slice-done.1
  243.8 11.6 %fusion.4 = f32[32,48,7,128]{3,1,2,0:T(8,128)S(1)} fusion(bf16[7,128,3584,1]{2,1,0,3:T(8,128)(2,1)S(1)} %bitcast.89, bf16[32,48,3584]{2,1,0:T(8,128)(2,1)S(1)} %copy-done), kind=kOutput, calls=%fused_computation.7 | convolution fusion | flops 9865003008 | bytes 22937600 | tf_op jit(solution)/shard_map/dot_general | solution.py:63
  255.5 1.9 subtract_convert_fusion
  257.4 3.6 fusion.9
  261.0 2.1 fusion.8
  263.2 2.3 fusion.7
  265.5 70.8 %all-gather.11.cloned.1.call-done = bf16[896,3584]{0,1:T(8,128)(2,1)} async-done(((bf16[896,448]{0,1:T(8,128)(2,1)}), bf16[896,3584]{0,1:T(8,128)(2,1)}) %all-gather.11.cloned.1.call-update) | async-done | bytes 6422544 | tf_op jit(solution)/shard_map/all_gather | solution.py:86
  336.3 5.5 %convolution_convert_fusion.1 = bf16[32,3584]{1,0:T(8,128)(2,1)} fusion(bf16[896,3584]{0,1:T(8,128)(2,1)} %all-gather.11.cloned.1.call-done, f32[4,8,7,128]{3,2,1,0:T(8,128)S(1)} %bitcast.91, f32[32]{0:T(128)S(1)} %convert_element_type.91), kind=kOutput, calls=%fused_computation.20 | convolution fusion | flops 205692928 | bytes 6766720 | tf_op jit(solution)/shard_map/dot_general | solution.py:84
  341.8 30.2 %all-reduce.2.cloned.1.call-done = bf16[32,3584]{1,0:T(8,128)(2,1)} async-done(((bf16[32,3584]{1,0:T(8,128)(2,1)}), bf16[32,3584]{1,0:T(8,128)(2,1)}) %all-reduce.2.cloned.1.call-update) | async-done | bytes 229392 | tf_op jit(solution)/shard_map/psum | solution.py:89
  372.0 1.2 multiply_reduce_fusion
  373.2 1.9 convolution_convert_fusion
  375.1 5.5 %all-to-all-start = ((bf16[8,4,3584]{2,1,0:T(4,128)(2,1)}), bf16[8,4,3584]{2,1,0:T(4,128)(2,1)S(1)}, u32[]{:S(2)}, u32[]{:S(2)}) async-start(bf16[8,4,3584]{2,1,0:T(4,128)(2,1)} %convolution_convert_fusion), calls=%async_computation | async-start | bytes 458752 | tf_op jit(solution)/shard_map/all_to_all | solution.py:119
  382.0 6.7 %all-to-all-done = bf16[8,4,3584]{2,1,0:T(4,128)(2,1)S(1)} async-done(((bf16[8,4,3584]{2,1,0:T(4,128)(2,1)}), bf16[8,4,3584]{2,1,0:T(4,128)(2,1)S(1)}, u32[]{:S(2)}, u32[]{:S(2)}) %all-to-all-start) | async-done | bytes 229408 | tf_op jit(solution)/shard_map/all_to_all | solution.py:119
  388.7 3.2 fusion.33
  391.9 9.2 %all_to_all.10 = bf16[8,4,512]{2,1,0:T(4,128)(2,1)S(1)} all-to-all(bf16[8,4,512]{2,1,0:T(4,128)(2,1)S(1)} %fusion.33), channel_id=1, replica_groups=mesh['dp'=8,'mp'=4] {'dp'}, dimensions={0} | all-to-all | bytes 65536 | tf_op jit(solution)/shard_map/all_to_all | solution.py:126
  401.2 0.8 convolution_bitcast_fusion
  (43 shorter events, 8.2 us)
Async XLA Ops:
  6.5 106.4 %all-gather.9.cloned.1.call-start = ((), (), s32[]{:S(2)}) async-start(), calls=%async_computation.4 | async-start | bytes 7225344 | tf_op jit(solution)/shard_map/all_gather | solution.py:59
  7.3 178.6 %all-gather.5.cloned.1.call-start = ((), (), s32[]{:S(2)}) async-start(), calls=%async_computation.2 | async-start | bytes 13762560 | tf_op jit(solution)/shard_map/all_gather | solution.py:49
  8.0 226.5 %all-gather.7.cloned.1.call-start = ((), (), s32[]{:S(2)}) async-start(), calls=%async_computation.3 | async-start | bytes 2064384 | tf_op jit(solution)/shard_map/all_gather | solution.py:60
  8.7 327.5 %all-gather.11.cloned.1.call-start = ((), (), s32[]{:S(2)}) async-start(), calls=%async_computation.5 | async-start | bytes 7225344 | tf_op jit(solution)/shard_map/all_gather | solution.py:86
  9.3 362.7 %all-reduce.2.cloned.1.call-start = ((), (), s32[]{:S(2)}) async-start(), calls=%async_computation.6 | async-start | bytes 458752 | tf_op jit(solution)/shard_map/psum | solution.py:89
  185.8 8.9 %copy-start.1 = (f32[3584]{0:T(1024)S(1)}, f32[3584]{0:T(1024)}, u32[]{:S(2)}) copy-start(f32[3584]{0:T(1024)} %param.12) | copy-start | bytes 43012
  194.8 47.4 %slice-start = ((s8[6422528]{0:T(1024)(128)(4,1)}), s8[2228224]{0:T(1024)(128)(4,1)S(1)}, s32[]{:S(2)}) async-start(s8[6422528]{0:T(1024)(128)(4,1)} %bitcast.87), calls=%async_computation.7 | async-start | bytes 4456448
  234.5 7.8 %copy-start = (bf16[32,48,3584]{2,1,0:T(8,128)(2,1)S(1)}, bf16[32,48,3584]{2,1,0:T(8,128)(2,1)}, u32[]{:S(2)}) copy-start(bf16[32,48,3584]{2,1,0:T(8,128)(2,1)} %fusion.3) | copy-start | bytes 33030148
  234.5 9.3 %slice-start.1 = ((s8[6422528]{0:T(1024)(128)(4,1)}), s8[4194304]{0:T(1024)(128)(4,1)S(1)}, s32[]{:S(2)}) async-start(s8[6422528]{0:T(1024)(128)(4,1)} %bitcast.87), calls=%async_computation.8 | async-start | bytes 8388608
  265.5 115.2 %copy-start.2 = (s32[8]{0:T(128)S(1)}, s32[8]{0:T(128)}, u32[]{:S(2)}) copy-start(s32[8]{0:T(128)} %param.19) | copy-start | bytes 100
  265.5 115.2 %copy-start.3 = (s32[8]{0:T(128)S(1)}, s32[8]{0:T(128)}, u32[]{:S(2)}) copy-start(s32[8]{0:T(128)} %param.20) | copy-start | bytes 100
  375.1 13.5 %all-to-all-start = ((bf16[8,4,3584]{2,1,0:T(4,128)(2,1)}), bf16[8,4,3584]{2,1,0:T(4,128)(2,1)S(1)}, u32[]{:S(2)}, u32[]{:S(2)}) async-start(bf16[8,4,3584]{2,1,0:T(4,128)(2,1)} %convolution_convert_fusion), calls=%async_computation | async-start | bytes 458752 | tf_op jit(solution)/shard_map/all_to_all | solution.py:119
Sparse Core Ops, SparseCore 0:
  9.5 103.3 all-gather.8
  114.5 71.2 all-gather.4
  188.0 46.4 all-gather.6
  236.6 99.6 all-gather.10
  341.9 30.0 all-reduce.1
where the time goes:
time: 409 us
  waiting for transfers between devices  299 us (73%)
  matrix products  36.3 us (9%)
  other arithmetic  33 us (8%)
  between operations  13.3 us (3%)
  local copies, waits for them, and re-layouts  11.5 us (3%)
  blocking collectives  9.24 us (2%)
  starting transfers between devices  5.66 us (1%)
    all_gather x1, waiting for transfers between devices, local(): lax.all_gather(w_query, 'dp', axis=0, tiled=True)  97.3 us
    all_gather x1, waiting for transfers between devices, local(): lax.all_gather(w_out, 'dp', axis=1, tiled=True)  70.8 us
    all_gather x1, waiting for transfers between devices, local(): gathered = lax.all_gather(tokens, 'mp', axis=2, tiled=True)  63.2 us
    psum x1, waiting for transfers between devices, local(): lax.psum(partial_out.astype(jnp.bfloat16), 'mp').astype(jnp.float32)  30.2 us
    all_gather x1, waiting for transfers between devices, local(): lax.all_gather(w_keyval, 'dp', axis=0, tiled=True)  28.8 us
    dot_general x1, matrix products, local(): jnp.dot(normed_flat, pieces[0], preferred_element_type=jnp.float32)  11.6 us
    convert_element_type x1, other arithmetic, local(): normed = (hidden * lax.rsqrt(jnp.mean(hidden * hidden, axis=-1, keepdims=...  11 us
    dot_general x1, local copies, waits for them, and re-layouts, local(): jnp.dot(normed_flat, pieces[0], preferred_element_type=jnp.float32)  9.72 us
  transfers between devices with their start and end apart: 6, of which 6 were waited for; matrix products, arithmetic and copies ran while one was open for 16% of the time, Pallas kernels for 0%

commit v1 on v0

--- a/solution.py
+++ b/solution.py
@@ -7,6 +7,23 @@
 HEAD_DIM = 128
 rope_base = 1000000.0
 logit_scale = 100.0
+
+
+def in_order(parts, dim):
+    lengths = list(parts.shape[1:])
+    lengths[dim] *= parts.shape[0]
+    return jnp.moveaxis(parts, 0, dim).reshape(lengths)
+
+
+def gather_around(shard, axis, dim):
+    size = lax.axis_size(axis)
+    forward = [(i, (i + 1) % size) for i in range(size)]
+    tiles = [shard]
+    while len(tiles) < size:
+        tiles.append(lax.ppermute(tiles[-1], axis, forward))
+    position = lax.axis_index(axis)
+    tiles = jnp.stack(tiles)[(position - jnp.arange(size)) % size]
+    return in_order(tiles, dim)
 
 
 def rotate(values, positions):
@@ -55,10 +72,7 @@
     normed_flat = normed.reshape(dialogs * seq_len, width)
     query_cols = w_query.shape[1]
     keyval_cols = w_keyval.shape[2]
-    pieces = (
-        lax.all_gather(w_query, "dp", axis=0, tiled=True),
-        lax.all_gather(w_keyval, "dp", axis=0, tiled=True),
-    )
+    pieces = (lax.all_gather(w_query, "dp", axis=0, tiled=True), gather_around(w_keyval, "dp", 0))
     keyval_piece = pieces[1].reshape(pieces[1].shape[0], 2 * keyval_cols)
     query_sum = jnp.dot(normed_flat, pieces[0], preferred_element_type=jnp.float32)
     keyval_sum = jnp.dot(normed_flat, keyval_piece, preferred_element_type=jnp.float32)

time: 409 us -> 386 us (0.944)
  waiting for transfers between devices: 299 us -> 274 us
  local copies, waits for them, and re-layouts: 11.5 us -> 17.5 us
  matrix products: 36.3 us -> 31.9 us
    ppermute x0 -> x7, waiting for transfers between devices: none -> 81.6 us  [gather_around(): tiles.append(lax.ppermute(tiles[-1], axis, forward))]
    all_gather x1, waiting for transfers between devices: 97.3 us -> 27.3 us  [local(): lax.all_gather(w_query, 'dp', axis=0, tiled=True)]
    all_gather x1 -> x0, waiting for transfers between devices: 28.8 us -> none  [local(): lax.all_gather(w_keyval, 'dp', axis=0, tiled=True)]
    all_gather x1, waiting for transfers between devices: 70.8 us -> 60.3 us  [local(): lax.all_gather(w_out, 'dp', axis=1, tiled=True)]
    gather x0 -> x1, local copies, waits for them, and re-layouts: none -> 5.35 us  [gather_around(): tiles = jnp.stack(tiles)[(position - jnp.arange(size)) % size]]
    dot_general x1, matrix products: 7.17 us -> 3.03 us  [local(): jnp.dot(normed_flat, keyval_piece, preferred_element_type=jnp.float32)]
  transfers between devices with their start and end apart: 6 -> 12, of which waited for: 6 -> 12; matrix products, arithmetic and copies ran while one was open for 16% -> 17% of each run, Pallas kernels for 0% -> 0%
where the time goes in v1:
time: 386 us
  waiting for transfers between devices  274 us (71%)
  matrix products  31.9 us (8%)
  other arithmetic  30.7 us (8%)
  local copies, waits for them, and re-layouts  17.5 us (5%)
  between operations  13.4 us (3%)
  blocking collectives  9.24 us (2%)
  starting transfers between devices  8.94 us (2%)
    ppermute x7, waiting for transfers between devices, gather_around(): tiles.append(lax.ppermute(tiles[-1], axis, forward))  81.6 us
    all_gather x1, waiting for transfers between devices, local(): gathered = lax.all_gather(tokens, 'mp', axis=2, tiled=True)  66.5 us
    all_gather x1, waiting for transfers between devices, local(): lax.all_gather(w_out, 'dp', axis=1, tiled=True)  60.3 us
    psum x1, waiting for transfers between devices, local(): lax.psum(partial_out.astype(jnp.bfloat16), 'mp').astype(jnp.float32)  30.2 us
    all_gather x1, waiting for transfers between devices, local(): lax.all_gather(w_query, 'dp', axis=0, tiled=True)  27.3 us
    dot_general x1, matrix products, local(): jnp.dot(normed_flat, pieces[0], preferred_element_type=jnp.float32)  11.6 us
    dot_general x1, local copies, waits for them, and re-layouts, local(): jnp.dot(normed_flat, pieces[0], preferred_element_type=jnp.float32)  9.54 us
    all_to_all x1, blocking collectives, local(): lax.all_to_all(jnp.where(live, logit_scale * dots * inverse_norm, 0.0).as...  9.24 us
  transfers between devices with their start and end apart: 12, of which 12 were waited for; matrix products, arithmetic and copies ran while one was open for 17% of the time, Pallas kernels for 0%

profile of v1, /device:TPU:0, one launch (start us, length us, event | category | flops | bytes accessed | tf_op | source)
XLA Modules:
  0.0 385.7 jit_solution(2076663594826325143)
XLA Ops:
  8.1 3.0 collective-permute-start
  15.3 2.8 fusion.6
  20.4 13.9 %collective-permute-done.1 = bf16[448,2,128]{2,1,0:T(2,128)(2,1)S(1)} collective-permute-done((bf16[448,2,128]{2,1,0:T(2,128)(2,1)S(1)}, bf16[448,2,128]{2,1,0:T(2,128)(2,1)S(1)}, u32[]{:S(2)}, u32[]{:S(2)}) %collective-permute-start.1) | collective-permute-done | bytes 229408 | tf_op jit(solution)/shard_map/ppermute | solution.py:23
  34.4 14.1 %collective-permute-done.2 = bf16[448,2,128]{2,1,0:T(2,128)(2,1)S(1)} collective-permute-done((bf16[448,2,128]{2,1,0:T(2,128)(2,1)S(1)}, bf16[448,2,128]{2,1,0:T(2,128)(2,1)S(1)}, u32[]{:S(2)}, u32[]{:S(2)}) %collective-permute-start.2) | collective-permute-done | bytes 229408 | tf_op jit(solution)/shard_map/ppermute | solution.py:23
  48.7 14.1 %collective-permute-done.3 = bf16[448,2,128]{2,1,0:T(2,128)(2,1)S(1)} collective-permute-done((bf16[448,2,128]{2,1,0:T(2,128)(2,1)S(1)}, bf16[448,2,128]{2,1,0:T(2,128)(2,1)S(1)}, u32[]{:S(2)}, u32[]{:S(2)}) %collective-permute-start.3) | collective-permute-done | bytes 229408 | tf_op jit(solution)/shard_map/ppermute | solution.py:23
  63.0 8.5 %collective-permute-done.4 = bf16[448,2,128]{2,1,0:T(2,128)(2,1)S(1)} collective-permute-done((bf16[448,2,128]{2,1,0:T(2,128)(2,1)S(1)}, bf16[448,2,128]{2,1,0:T(2,128)(2,1)S(1)}, u32[]{:S(2)}, u32[]{:S(2)}) %collective-permute-start.4) | collective-permute-done | bytes 229408 | tf_op jit(solution)/shard_map/ppermute | solution.py:23
  71.7 15.0 %collective-permute-done.5 = bf16[448,2,128]{2,1,0:T(2,128)(2,1)S(1)} collective-permute-done((bf16[448,2,128]{2,1,0:T(2,128)(2,1)S(1)}, bf16[448,2,128]{2,1,0:T(2,128)(2,1)S(1)}, u32[]{:S(2)}, u32[]{:S(2)}) %collective-permute-start.5) | collective-permute-done | bytes 229408 | tf_op jit(solution)/shard_map/ppermute | solution.py:23
  86.9 14.7 %collective-permute-done.6 = bf16[448,2,128]{2,1,0:T(2,128)(2,1)S(1)} collective-permute-done((bf16[448,2,128]{2,1,0:T(2,128)(2,1)S(1)}, bf16[448,2,128]{2,1,0:T(2,128)(2,1)S(1)}, u32[]{:S(2)}, u32[]{:S(2)}) %collective-permute-start.6) | collective-permute-done | bytes 229408 | tf_op jit(solution)/shard_map/ppermute | solution.py:23
  101.9 5.3 %gather_fusion = bf16[8,448,2,128]{3,2,1,0:T(2,128)(2,1)} fusion(bf16[8,448,2,128]{3,2,1,0:T(2,128)(2,1)S(1)} %bitcast_dynamic-update-slice_fusion, s32[1024]{0:T(1024)S(1)} %pad_clamp_fusion), kind=kCustom, calls=%fused_computation | custom fusion | bytes 3670048 | tf_op jit(solution)/shard_map/gather | solution.py:25
  107.2 27.3 %all-gather.6.cloned.1.call-done = bf16[3584,896]{1,0:T(8,128)(2,1)} async-done(((bf16[448,896]{1,0:T(8,128)(2,1)}), bf16[3584,896]{1,0:T(8,128)(2,1)}) %all-gather.6.cloned.1.call-update) | async-done | bytes 6422544 | tf_op jit(solution)/shard_map/all_gather | solution.py:75
  134.5 9.5 %copy.20 = bf16[896,3584]{1,0:T(8,128)(2,1)} copy(bf16[896,3584]{0,1:T(8,128)(2,1)} %bitcast.105) | data formatting | bytes 12845056 | tf_op jit(solution)/shard_map/dot_general | solution.py:77
  144.1 66.5 %all-gather.4.cloned.1.call-done = bf16[32,48,3584]{2,1,0:T(8,128)(2,1)} async-done(((bf16[32,48,896]{2,1,0:T(8,128)(2,1)}), bf16[32,48,3584]{2,1,0:T(8,128)(2,1)}) %all-gather.4.cloned.1.call-update) | async-done | bytes 11010064 | tf_op jit(solution)/shard_map/all_gather | solution.py:66
  210.6 8.9 %fusion = (f32[32,3584]{1,0:T(8,128)S(1)}, f32[32,48]{1,0:T(8,128)S(1)}) fusion(bf16[32,48,3584]{2,1,0:T(8,128)(2,1)} %all-gather.4.cloned.1.call-done, f32[32,48]{1,0:T(8,128)S(1)} %get-tuple-element.14), kind=kLoop, calls=%fused_computation.4 | loop fusion | flops 27408896 | bytes 11481088 | tf_op jit(solution)/shard_map/reduce_sum | solution.py:96
  219.5 8.4 %fusion.3 = bf16[32,48,3584]{2,1,0:T(8,128)(2,1)S(1)} fusion(bf16[32,48,3584]{2,1,0:T(8,128)(2,1)} %all-gather.4.cloned.1.call-done, f32[3584]{0:T(1024)S(1)} %copy-done.1, f32[32,48]{1,0:T(8,128)S(1)} %add_rsqrt_fusion), kind=kLoop, calls=%fused_computation.7 | loop fusion | flops 22020096 | bytes 22040576 | tf_op jit(solution)/shard_map/convert_element_type | solution.py:71
  228.0 3.0 fusion.22
  231.5 11.6 %fusion.4 = f32[32,48,7,128]{3,1,2,0:T(8,128)S(1)} fusion(bf16[7,128,3584,1]{2,1,0,3:T(8,128)(2,1)S(1)} %bitcast.108, bf16[32,48,3584]{2,1,0:T(8,128)(2,1)S(1)} %fusion.3), kind=kOutput, calls=%fused_computation.8 | convolution fusion | flops 9865003008 | bytes 22937600 | tf_op jit(solution)/shard_map/dot_general | solution.py:77
  245.3 3.4 fusion.9
  253.2 60.3 %all-gather.8.cloned.1.call-done = bf16[896,3584]{0,1:T(8,128)(2,1)} async-done(((bf16[896,448]{0,1:T(8,128)(2,1)}), bf16[896,3584]{0,1:T(8,128)(2,1)}) %all-gather.8.cloned.1.call-update) | async-done | bytes 6422544 | tf_op jit(solution)/shard_map/all_gather | solution.py:100
  313.4 5.5 %convolution_convert_fusion.1 = bf16[32,3584]{1,0:T(8,128)(2,1)} fusion(bf16[896,3584]{0,1:T(8,128)(2,1)} %all-gather.8.cloned.1.call-done, f32[4,8,7,128]{3,2,1,0:T(8,128)S(1)} %bitcast.111, f32[32]{0:T(128)S(1)} %convert_element_type.91), kind=kOutput, calls=%fused_computation.21 | convolution fusion | flops 205692928 | bytes 6766720 | tf_op jit(solution)/shard_map/dot_general | solution.py:98
  319.0 30.2 %all-reduce.2.cloned.1.call-done = bf16[32,3584]{1,0:T(8,128)(2,1)} async-done(((bf16[32,3584]{1,0:T(8,128)(2,1)}), bf16[32,3584]{1,0:T(8,128)(2,1)}) %all-reduce.2.cloned.1.call-update) | async-done | bytes 229392 | tf_op jit(solution)/shard_map/psum | solution.py:103
  352.4 5.5 %all-to-all-start = ((bf16[8,4,3584]{2,1,0:T(4,128)(2,1)}), bf16[8,4,3584]{2,1,0:T(4,128)(2,1)S(1)}, u32[]{:S(2)}, u32[]{:S(2)}) async-start(bf16[8,4,3584]{2,1,0:T(4,128)(2,1)} %convolution_convert_fusion), calls=%async_computation | async-start | bytes 458752 | tf_op jit(solution)/shard_map/all_to_all | solution.py:133
  359.2 6.7 %all-to-all-done = bf16[8,4,3584]{2,1,0:T(4,128)(2,1)S(1)} async-done(((bf16[8,4,3584]{2,1,0:T(4,128)(2,1)}), bf16[8,4,3584]{2,1,0:T(4,128)(2,1)S(1)}, u32[]{:S(2)}, u32[]{:S(2)}) %all-to-all-start) | async-done | bytes 229408 | tf_op jit(solution)/shard_map/all_to_all | solution.py:133
  365.9 3.2 fusion.33
  369.1 9.2 %all_to_all.10 = bf16[8,4,512]{2,1,0:T(4,128)(2,1)S(1)} all-to-all(bf16[8,4,512]{2,1,0:T(4,128)(2,1)S(1)} %fusion.33), channel_id=1, replica_groups=mesh['dp'=8,'mp'=4] {'dp'}, dimensions={0} | all-to-all | bytes 65536 | tf_op jit(solution)/shard_map/all_to_all | solution.py:140
  (65 shorter events, 21.4 us)
Async XLA Ops:
  6.5 128.0 %all-gather.6.cloned.1.call-start = ((), (), s32[]{:S(2)}) async-start(), calls=%async_computation.3 | async-start | bytes 7225344 | tf_op jit(solution)/shard_map/all_gather | solution.py:75
  7.3 203.3 %all-gather.4.cloned.1.call-start = ((), (), s32[]{:S(2)}) async-start(), calls=%async_computation.2 | async-start | bytes 13762560 | tf_op jit(solution)/shard_map/all_gather | solution.py:66
  8.0 305.4 %all-gather.8.cloned.1.call-start = ((), (), s32[]{:S(2)}) async-start(), calls=%async_computation.4 | async-start | bytes 7225344 | tf_op jit(solution)/shard_map/all_gather | solution.py:100
  8.1 11.8 %collective-permute-start = (bf16[448,2,128]{2,1,0:T(2,128)(2,1)}, bf16[448,2,128]{2,1,0:T(2,128)(2,1)S(1)}, u32[]{:S(2)}, u32[]{:S(2)}) collective-permute-start(bf16[448,2,128]{2,1,0:T(2,128)(2,1)} %param.14), channel_id=1, source_target_pairs={{0,4},{4,8},{8,12},{12,16},{16,20},{20,24},{24,28},{28,0},{1,5},{5... | collective-permute-start | bytes 688136 | tf_op jit(solution)/shard_map/ppermute | solution.py:23
  11.1 338.1 %all-reduce.2.cloned.1.call-start = ((), (), s32[]{:S(2)}) async-start(), calls=%async_computation.5 | async-start | bytes 458752 | tf_op jit(solution)/shard_map/psum | solution.py:103
  19.9 14.3 %collective-permute-start.1 = (bf16[448,2,128]{2,1,0:T(2,128)(2,1)S(1)}, bf16[448,2,128]{2,1,0:T(2,128)(2,1)S(1)}, u32[]{:S(2)}, u32[]{:S(2)}) collective-permute-start(bf16[448,2,128]{2,1,0:T(2,128)(2,1)S(1)} %collective-permute-done), channel_id=1, source_target_pairs={{0,4},{4,8},{8,12},{12,16},{16,20},{20,24},{24,28},{28,0},{1,5},{5... | collective-permute-start | bytes 688136 | tf_op jit(solution)/shard_map/ppermute | solution.py:23
  34.2 14.3 %collective-permute-start.2 = (bf16[448,2,128]{2,1,0:T(2,128)(2,1)S(1)}, bf16[448,2,128]{2,1,0:T(2,128)(2,1)S(1)}, u32[]{:S(2)}, u32[]{:S(2)}) collective-permute-start(bf16[448,2,128]{2,1,0:T(2,128)(2,1)S(1)} %collective-permute-done.1), channel_id=1, source_target_pairs={{0,4},{4,8},{8,12},{12,16},{16,20},{20,24},{24,28},{28,0},{1,5},{5... | collective-permute-start | bytes 688136 | tf_op jit(solution)/shard_map/ppermute | solution.py:23
  48.5 14.3 %collective-permute-start.3 = (bf16[448,2,128]{2,1,0:T(2,128)(2,1)S(1)}, bf16[448,2,128]{2,1,0:T(2,128)(2,1)S(1)}, u32[]{:S(2)}, u32[]{:S(2)}) collective-permute-start(bf16[448,2,128]{2,1,0:T(2,128)(2,1)S(1)} %collective-permute-done.2), channel_id=1, source_target_pairs={{0,4},{4,8},{8,12},{12,16},{16,20},{20,24},{24,28},{28,0},{1,5},{5... | collective-permute-start | bytes 688136 | tf_op jit(solution)/shard_map/ppermute | solution.py:23
  62.8 8.7 %collective-permute-start.4 = (bf16[448,2,128]{2,1,0:T(2,128)(2,1)S(1)}, bf16[448,2,128]{2,1,0:T(2,128)(2,1)S(1)}, u32[]{:S(2)}, u32[]{:S(2)}) collective-permute-start(bf16[448,2,128]{2,1,0:T(2,128)(2,1)S(1)} %collective-permute-done.3), channel_id=1, source_target_pairs={{0,4},{4,8},{8,12},{12,16},{16,20},{20,24},{24,28},{28,0},{1,5},{5... | collective-permute-start | bytes 688136 | tf_op jit(solution)/shard_map/ppermute | solution.py:23
  71.5 15.2 %collective-permute-start.5 = (bf16[448,2,128]{2,1,0:T(2,128)(2,1)S(1)}, bf16[448,2,128]{2,1,0:T(2,128)(2,1)S(1)}, u32[]{:S(2)}, u32[]{:S(2)}) collective-permute-start(bf16[448,2,128]{2,1,0:T(2,128)(2,1)S(1)} %collective-permute-done.4), channel_id=1, source_target_pairs={{0,4},{4,8},{8,12},{12,16},{16,20},{20,24},{24,28},{28,0},{1,5},{5... | collective-permute-start | bytes 688136 | tf_op jit(solution)/shard_map/ppermute | solution.py:23
  86.7 14.9 %collective-permute-start.6 = (bf16[448,2,128]{2,1,0:T(2,128)(2,1)S(1)}, bf16[448,2,128]{2,1,0:T(2,128)(2,1)S(1)}, u32[]{:S(2)}, u32[]{:S(2)}) collective-permute-start(bf16[448,2,128]{2,1,0:T(2,128)(2,1)S(1)} %collective-permute-done.5), channel_id=1, source_target_pairs={{0,4},{4,8},{8,12},{12,16},{16,20},{20,24},{24,28},{28,0},{1,5},{5... | collective-permute-start | bytes 688136 | tf_op jit(solution)/shard_map/ppermute | solution.py:23
  210.6 8.9 %copy-start.1 = (f32[3584]{0:T(1024)S(1)}, f32[3584]{0:T(1024)}, u32[]{:S(2)}) copy-start(f32[3584]{0:T(1024)} %param.12) | copy-start | bytes 43012
  219.5 8.4 %copy-start = (bf16[8,448,2,128]{3,2,1,0:T(2,128)(2,1)S(1)}, bf16[8,448,2,128]{3,2,1,0:T(2,128)(2,1)}, u32[]{:S(2)}) copy-start(bf16[8,448,2,128]{3,2,1,0:T(2,128)(2,1)} %gather_fusion) | copy-start | bytes 5505028
  219.5 11.9 %slice-start = ((s8[6422528]{0:T(1024)(128)(4,1)}), s8[4194304]{0:T(1024)(128)(4,1)S(1)}, s32[]{:S(2)}) async-start(s8[6422528]{0:T(1024)(128)(4,1)} %bitcast.106), calls=%async_computation.6 | async-start | bytes 8388608
  227.9 3.5 slice-start.1
  253.1 104.7 %copy-start.2 = (s32[8]{0:T(128)S(1)}, s32[8]{0:T(128)}, u32[]{:S(2)}) copy-start(s32[8]{0:T(128)} %param.19) | copy-start | bytes 100
  253.2 104.7 %copy-start.3 = (s32[8]{0:T(128)S(1)}, s32[8]{0:T(128)}, u32[]{:S(2)}) copy-start(s32[8]{0:T(128)} %param.20) | copy-start | bytes 100
  352.4 13.5 %all-to-all-start = ((bf16[8,4,3584]{2,1,0:T(4,128)(2,1)}), bf16[8,4,3584]{2,1,0:T(4,128)(2,1)S(1)}, u32[]{:S(2)}, u32[]{:S(2)}) async-start(bf16[8,4,3584]{2,1,0:T(4,128)(2,1)} %convolution_convert_fusion), calls=%async_computation | async-start | bytes 458752 | tf_op jit(solution)/shard_map/all_to_all | solution.py:133
Sparse Core Ops, SparseCore 0:
  9.5 124.9 all-gather.5
  136.1 74.4 all-gather.3
  212.8 100.6 all-gather.7
  319.1 30.0 all-reduce.1
